TPU v7x, 512 devices: a whole 4x8x8 slice. The times are simulated.
512 devices in a mesh: ctx: 128 (over y, z, x_lo), tp: 4 (over x_hi, core).
Axes of the slice: x: 4 (x_hi: 2, x_lo: 2; x = x_hi * 2 + x_lo), y: 8, z: 8, core: 2. Of those that a mesh axis runs over, the one named last changes fastest.
Arguments:
- features: bfloat16 [3, 2048, 16384], P(None, 'tp', 'ctx'), may hold values from -6 to 6
- short_taps: float32 [3, 3, 2048], P(None, None, 'tp'), may hold values from -3 to 3
- filters: bfloat16 [128, 16384], P('tp'), may hold values from -2 to 2
- skip_gain: float32 [2048], P('tp'), may hold values from -4 to 4
- out_weight: bfloat16 [2048, 2048], P('tp'), may hold values from -0.125 to 0.125
Outputs:
- block_out: bfloat16 [2048, 16384], P('tp', 'ctx')
All inputs are finite; a program needn't handle non-finite values.
Results may differ from a plain program's by a relative error of at most 0.009.
Values may be sent and summed in bfloat16 or wider, within the bound.
No kernel may reach another device: no remote copies, remote signals or barrier semaphores. Data moves between devices by JAX's collectives and lax.ppermute only.
A program may use at most 64 MiB of HBM per device.

v0:
```python
import math
import jax
import jax.numpy as jnp
from jax import lax
from jax.sharding import PartitionSpec as P

GROUP = 16
highest = lax.Precision.HIGHEST


def from_behind(value, axis, steps):
    count = lax.axis_size(axis)
    initial, last = (max(0, -steps), min(count, count - steps))
    return lax.ppermute(value, axis, [(source, source + steps) for source in range(initial, last)])


def left_product(matrix, stacked):
    return jnp.einsum("kn,bns->bks", matrix, stacked, precision=highest)


def right_product(stacked, matrix):
    return jnp.einsum("bks,st->bkt", stacked, matrix, precision=highest)


def split_length(total_len):
    row_count = 2
    for candidate in range(2, math.isqrt(total_len) + 1, 2):
        if total_len % candidate == 0:
            row_count = candidate
    return (row_count, total_len // row_count)


def dft_tables(row_count, col_count):
    total_len = row_count * col_count
    row_index = jnp.arange(row_count, dtype=jnp.int32)
    col_index = jnp.arange(col_count, dtype=jnp.int32)
    row_angle = (row_index[:, None] * row_index[None, :] % row_count).astype(jnp.float32) * (
        2.0 * math.pi / row_count
    )
    col_angle = (col_index[:, None] * col_index[None, :] % col_count).astype(jnp.float32) * (
        2.0 * math.pi / col_count
    )
    twist_angle = (row_index[:, None] * col_index[None, :] % total_len).astype(jnp.float32) * (
        2.0 * math.pi / total_len
    )
    return (
        jnp.cos(row_angle),
        jnp.sin(row_angle),
        jnp.cos(col_angle),
        jnp.sin(col_angle),
        jnp.cos(twist_angle),
        jnp.sin(twist_angle),
    )


def forward_dft(signal, tables):
    cos_row, sin_row, cos_col, sin_col, cos_twist, sin_twist = tables
    half_rows = signal.shape[1]
    first_real = left_product(cos_row[:, :half_rows], signal)
    first_imag = -left_product(sin_row[:, :half_rows], signal)
    twist_real = first_real * cos_twist + first_imag * sin_twist
    twist_imag = first_imag * cos_twist - first_real * sin_twist
    spec_real = right_product(twist_real, cos_col) + right_product(twist_imag, sin_col)
    spec_imag = right_product(twist_imag, cos_col) - right_product(twist_real, sin_col)
    return (spec_real, spec_imag)


def inverse_dft(spec_real, spec_imag, tables, half_rows):
    cos_row, sin_row, cos_col, sin_col, cos_twist, sin_twist = tables
    total_len = cos_row.shape[0] * cos_col.shape[0]
    middle_real = right_product(spec_real, cos_col) - right_product(spec_imag, sin_col)
    middle_imag = right_product(spec_imag, cos_col) + right_product(spec_real, sin_col)
    turned_real = middle_real * cos_twist - middle_imag * sin_twist
    turned_imag = middle_imag * cos_twist + middle_real * sin_twist
    signal = left_product(cos_row[:half_rows, :], turned_real) - left_product(
        sin_row[:half_rows, :], turned_imag
    )
    return signal / total_len


def local(features, short_taps, filters, skip_gain, out_weight):
    taps_count = short_taps.shape[0]
    chan_tp = features.shape[1]
    tok_local = features.shape[2]
    ctx_count = lax.axis_size("ctx")
    chan_dev = chan_tp // ctx_count
    group_dev = max(1, chan_dev // GROUP)
    per_group = chan_dev // group_dev
    seq_len = tok_local * ctx_count
    row_count, col_count = split_length(2 * seq_len)
    half_rows = row_count // 2
    tables = dft_tables(row_count, col_count)
    ctx_rank = lax.axis_index("ctx")
    kernel_rows = lax.dynamic_slice_in_dim(filters, ctx_rank * chan_dev // GROUP, group_dev, 0)
    kernel_real, kernel_imag = forward_dft(
        kernel_rows.astype(jnp.float32).reshape(group_dev, half_rows, col_count), tables
    )
    previous = from_behind(features[:, :, tok_local - (taps_count - 1) :], "ctx", 1)
    extended = jnp.concatenate([previous, features], axis=2).astype(jnp.float32)
    conv_all = jnp.zeros(features.shape, jnp.float32)
    for offset in range(taps_count):
        begin_at = taps_count - 1 - offset
        conv_all = (
            conv_all
            + short_taps[offset][:, :, None] * extended[:, :, begin_at : begin_at + tok_local]
        )
    query_conv = conv_all[0]
    product = (conv_all[1] * conv_all[2]).astype(jnp.bfloat16)
    gathered = lax.all_to_all(product, "ctx", split_axis=0, concat_axis=1, tiled=True)
    signal = gathered.astype(jnp.float32)
    sig_real, sig_imag = forward_dft(signal.reshape(chan_dev, half_rows, col_count), tables)
    four_shape = (group_dev, per_group, row_count, col_count)
    sig_real = sig_real.reshape(four_shape)
    sig_imag = sig_imag.reshape(four_shape)
    kernel_wide_real = kernel_real[:, None]
    kernel_wide_imag = kernel_imag[:, None]
    prod_real = (sig_real * kernel_wide_real - sig_imag * kernel_wide_imag).reshape(
        chan_dev, row_count, col_count
    )
    prod_imag = (sig_real * kernel_wide_imag + sig_imag * kernel_wide_real).reshape(
        chan_dev, row_count, col_count
    )
    longconv = inverse_dft(prod_real, prod_imag, tables, half_rows).reshape(chan_dev, seq_len)
    skip_local = lax.dynamic_slice_in_dim(skip_gain, ctx_rank * chan_dev, chan_dev, 0)
    long_mix = (longconv + skip_local[:, None] * signal).astype(jnp.bfloat16)
    restored = lax.all_to_all(long_mix, "ctx", split_axis=1, concat_axis=0, tiled=True)
    gated = (query_conv * restored.astype(jnp.float32)).astype(jnp.bfloat16)
    return lax.psum_scatter(
        lax.dot_general(
            out_weight, gated, (((0,), (0,)), ((), ())), preferred_element_type=jnp.float32
        ).astype(jnp.bfloat16),
        "tp",
        scatter_dimension=0,
        tiled=True,
    )


def solution(mesh):
    placed = (P(None, "tp", "ctx"), P(None, None, "tp"), P("tp", None), P("tp"), P("tp", None))
    return jax.shard_map(
        local, mesh=mesh, in_specs=placed, out_specs=P("tp", "ctx"), check_vma=False
    )
```

profile of v0, /device:TPU:1, one launch (start us, length us, event | category | flops | bytes accessed | tf_op | source)
XLA Modules:
  0.0 139.9 jit_solution(3832880754229626524)
XLA Ops:
  6.5 0.0 copy-start
  6.5 2.1 %slice.49 = bf16[3,512,2]{2,1,0:T(8,128)(2,1)} slice(bf16[3,512,128]{2,1,0:T(8,128)(2,1)} %param.5), slice={[0:3], [0:512], [126:128]} | slice | bytes 12288 | tf_op jit(solution)/shard_map/slice | solution.py:98
  8.6 3.9 %collective-permute-start = (bf16[3,512,2]{2,1,0:T(8,128)(2,1)}, bf16[3,512,2]{2,1,0:T(8,128)(2,1)S(1)}, u32[]{:S(2)}, u32[]{:S(2)}) collective-permute-start(bf16[3,512,2]{2,1,0:T(8,128)(2,1)} %slice.49), channel_id=1, source_target_pairs={{0,4},{4,8},{8,12},{12,16},{16,20},{20,24},{24,28},{28,32},{32,36}... | collective-permute-start | bytes 18440 | tf_op jit(solution)/shard_map/ppermute | solution.py:14
  12.6 0.3 fusion.85
  12.8 0.0 copy-start.2
  12.8 0.3 fusion.84
  13.1 0.0 copy-start.4
  13.1 1.2 dynamic-slice_reduce_fusion
  14.3 0.3 fusion.4
  14.6 0.0 copy-start.6
  14.6 0.3 convolution_bitcast_fusion.1
  14.9 0.0 copy-done.4
  14.9 0.0 copy-start.7
  14.9 1.8 %fusion.46 = f32[128,256]{1,0:T(8,128)S(1)} fusion(f32[1,128,256]{1,2,0:T(8,128)S(1)} %convolution_bitcast_fusion.1, f32[1,128,256]{1,2,0:T(8,128)S(1)} %fusion.4), kind=kOutput, calls=%fused_computation.77 | convolution fusion | flops 102137856 | bytes 393216 | tf_op jit(solution)/shard_map/bks,st->bkt/dot_general | solution.py:22
  16.7 0.0 copy-start.8
  16.7 0.0 copy-start.1
  16.7 2.5 %fusion.50 = f32[128,256]{1,0:T(8,128)} fusion(f32[1,128,256]{1,2,0:T(8,128)S(1)} %fusion.4, f32[1,128,256]{1,2,0:T(8,128)S(1)} %convolution_bitcast_fusion.1), kind=kOutput, calls=%fused_computation.81 | convolution fusion | flops 102137856 | bytes 393216 | tf_op jit(solution)/shard_map/bks,st->bkt/dot_general | solution.py:22
  19.2 0.0 copy-done.2
  19.2 0.0 copy-done.6
  19.2 0.0 copy-done.7
  19.2 1.8 %convolution_subtract_fusion.3 = f32[128,256]{1,0:T(8,128)S(1)} fusion(f32[128,256]{1,0:T(8,128)S(1)} %fusion.46, f32[1,128,256]{1,2,0:T(8,128)S(1)} %fusion.4, f32[1,128,256]{1,2,0:T(8,128)S(1)} %convolution_bitcast_fusion.1), kind=kOutput, calls=%fused_computation.12 | convolution fusion | flops 102170624 | bytes 524288 | tf_op jit(solution)/shard_map/bks,st->bkt/dot_general | solution.py:22
  21.0 0.0 copy-done.8
  21.0 0.0 collective-permute-done
  21.0 0.0 copy-done.1
  21.1 0.3 maximum_convert_fusion
  21.4 1.2 fusion.5
  22.6 0.7 fusion.17
  23.3 20.1 %all-to-all-start = ((bf16[128,4,128]{2,1,0:T(4,128)(2,1)}), bf16[128,4,128]{2,1,0:T(4,128)(2,1)S(1)}, u32[]{:S(2)}, u32[]{:S(2)}) async-start(bf16[128,4,128]{2,1,0:T(4,128)(2,1)} %bitcast.4), calls=%async_computation | async-start | bytes 262144 | tf_op jit(solution)/shard_map/all_to_all | solution.py:109
  43.3 0.2 reduce-scatter.2.cloned.1.call-start
  43.6 0.5 fusion.77
  44.1 0.8 dynamic_slice.7
  44.9 2.8 %convolution_add_fusion.2 = f32[128,256]{1,0:T(8,128)S(1)} fusion(f32[128,256]{1,0:T(8,128)} %fusion.50, f32[1,128,256]{1,2,0:T(8,128)} %copy-done.7, f32[1,128,256]{1,2,0:T(8,128)} %copy-done.6), kind=kOutput, calls=%fused_computation.13 | convolution fusion | flops 102170624 | bytes 524288 | tf_op jit(solution)/shard_map/bks,st->bkt/dot_general | solution.py:22
  47.7 6.8 %all-to-all-done = bf16[128,4,128]{2,1,0:T(4,128)(2,1)S(1)} async-done(((bf16[128,4,128]{2,1,0:T(4,128)(2,1)}), bf16[128,4,128]{2,1,0:T(4,128)(2,1)S(1)}, u32[]{:S(2)}, u32[]{:S(2)}) %all-to-all-start) | async-done | bytes 131104 | tf_op jit(solution)/shard_map/all_to_all | solution.py:109
  54.5 0.7 copy.68
  55.2 1.6 %reshape.145 = bf16[4,64,256]{2,1,0:T(8,128)(2,1)} reshape(bf16[4,128,128]{2,1,0:T(8,128)(2,1)} %bitcast.84) | data formatting | bytes 262144 | tf_op jit(solution)/shard_map/reshape | solution.py:111
  56.8 1.3 fusion.1
  58.2 1.3 convolution_bitcast_fusion
  59.5 1.9 %fusion.28 = f32[4,128,256]{2,1,0:T(8,128)S(1)} fusion(f32[4,128,256]{1,2,0:T(8,128)S(1)} %convolution_bitcast_fusion, f32[4,128,256]{1,2,0:T(8,128)S(1)} %fusion.1, f32[128,256]{0,1:T(8,128)S(1)} %get-tuple-element.8, f32[128,256]{0,1:T(8,128)S(1)} %get-tuple-element.9), kind=kOutput, calls=%fused_computation.53 | convolution fusion | flops 403963904 | bytes 1835008 | tf_op jit(solution)/shard_map/bks,st->bkt/dot_general | solution.py:22
  61.4 1.9 %fusion.30 = f32[4,128,256]{2,1,0:T(8,128)S(1)} fusion(f32[4,128,256]{1,2,0:T(8,128)S(1)} %fusion.1, f32[4,128,256]{1,2,0:T(8,128)S(1)} %convolution_bitcast_fusion, f32[128,256]{0,1:T(8,128)S(1)} %get-tuple-element.8, f32[128,256]{0,1:T(8,128)S(1)} %get-tuple-element.9), kind=kOutput, calls=%fused_computation.55 | convolution fusion | flops 403963904 | bytes 1835008 | tf_op jit(solution)/shard_map/bks,st->bkt/dot_general | solution.py:22
  63.3 1.9 %convolution_subtract_fusion.1 = f32[4,128,256]{2,1,0:T(8,128)S(1)} fusion(f32[4,128,256]{2,1,0:T(8,128)S(1)} %fusion.28, f32[4,128,256]{1,2,0:T(8,128)S(1)} %fusion.1, f32[4,128,256]{1,2,0:T(8,128)S(1)} %convolution_bitcast_fusion, f32[128,256]{0,1:T(8,128)S(1)} %get-tuple-element.8, f32[128,256]{0,1:T(8,128)S(1)} %get-tuple-element.9), kind=kOutput, calls=%fused_computation.7 | convolution fusion | flops 404094976 | bytes 2359296 | tf_op jit(solution)/shard_map/bks,st->bkt/dot_general | solution.py:22
  65.2 1.9 %convolution_add_fusion.1 = f32[4,128,256]{2,1,0:T(8,128)S(1)} fusion(f32[4,128,256]{2,1,0:T(8,128)S(1)} %fusion.30, f32[4,128,256]{1,2,0:T(8,128)S(1)} %convolution_bitcast_fusion, f32[4,128,256]{1,2,0:T(8,128)S(1)} %fusion.1, f32[128,256]{0,1:T(8,128)S(1)} %get-tuple-element.8, f32[128,256]{0,1:T(8,128)S(1)} %get-tuple-element.9), kind=kOutput, calls=%fused_computation.8 | convolution fusion | flops 404094976 | bytes 2359296 | tf_op jit(solution)/shard_map/bks,st->bkt/dot_general | solution.py:22
  67.0 1.9 %fusion.24 = f32[4,128,256]{1,2,0:T(8,128)S(1)} fusion(f32[4,128,256]{2,1,0:T(8,128)S(1)} %convolution_subtract_fusion.1, f32[4,128,256]{2,1,0:T(8,128)S(1)} %convolution_add_fusion.1, f32[128,256]{1,0:T(8,128)S(1)} %convolution_subtract_fusion.3, f32[128,256]{1,0:T(8,128)S(1)} %convolution_add_fusion.2), kind=kOutput, calls=%fused_computation.49 | convolution fusion | flops 403963904 | bytes 1835008 | tf_op jit(solution)/shard_map/bks,st->bkt/dot_general | solution.py:22
  69.0 1.7 %fusion.26 = f32[4,128,256]{1,2,0:T(8,128)S(1)} fusion(f32[4,128,256]{2,1,0:T(8,128)S(1)} %convolution_subtract_fusion.1, f32[4,128,256]{2,1,0:T(8,128)S(1)} %convolution_add_fusion.1, f32[128,256]{1,0:T(8,128)S(1)} %convolution_subtract_fusion.3, f32[128,256]{1,0:T(8,128)S(1)} %convolution_add_fusion.2), kind=kOutput, calls=%fused_computation.51 | convolution fusion | flops 403963904 | bytes 1835008 | tf_op jit(solution)/shard_map/bks,st->bkt/dot_general | solution.py:22
  70.7 1.7 %convolution_add_fusion = f32[4,128,256]{1,2,0:T(8,128)S(1)} fusion(f32[4,128,256]{1,2,0:T(8,128)S(1)} %fusion.24, f32[4,128,256]{2,1,0:T(8,128)S(1)} %convolution_subtract_fusion.1, f32[4,128,256]{2,1,0:T(8,128)S(1)} %convolution_add_fusion.1, f32[128,256]{1,0:T(8,128)S(1)} %convolution_subtract_fusion.3, f32[128,256]{1,0:T(8,128)S(1)} %convolution_add_fusion.2), kind=kOutput, calls=%fused_computation.5 | convolution fusion | flops 404094976 | bytes 2359296 | tf_op jit(solution)/shard_map/bks,st->bkt/dot_general | solution.py:22
  72.4 0.0 copy-start.3
  72.4 0.0 copy-start.5
  72.4 1.7 %convolution_subtract_fusion = f32[4,128,256]{1,2,0:T(8,128)S(1)} fusion(f32[4,128,256]{1,2,0:T(8,128)S(1)} %fusion.26, f32[4,128,256]{2,1,0:T(8,128)S(1)} %convolution_subtract_fusion.1, f32[4,128,256]{2,1,0:T(8,128)S(1)} %convolution_add_fusion.1, f32[128,256]{1,0:T(8,128)S(1)} %convolution_subtract_fusion.3, f32[128,256]{1,0:T(8,128)S(1)} %convolution_add_fusion.2), kind=kOutput, calls=%fused_computation.6 | convolution fusion | flops 404094976 | bytes 2359296 | tf_op jit(solution)/shard_map/bks,st->bkt/dot_general | solution.py:22
  74.1 0.0 copy-done.3
  74.2 0.8 fusion.10
  74.9 0.0 copy-done.5
  74.9 1.5 %fusion.3 = f32[4,64,256]{2,1,0:T(8,128)} fusion(f32[4,256,64]{1,2,0:T(8,128)S(1)} %fusion.10, f32[4,128,256]{1,2,0:T(8,128)S(1)} %convolution_subtract_fusion, f32[4,128,256]{1,2,0:T(8,128)S(1)} %convolution_add_fusion, f32[128,256]{0,1:T(8,128)S(1)} %get-tuple-element.8, f32[128,256]{0,1:T(8,128)S(1)} %get-tuple-element.9, f32[128,128]{0,1:T(8,128)S(1)} %copy-done.5), kind=kOutput, calls=%fused_computation.11 | convolution fusion | flops 101187584 | bytes 1900544 | tf_op jit(solution)/shard_map/kn,bns->bks/dot_general | solution.py:18
  76.4 1.0 reshape.149
  77.4 0.1 add_convert_fusion
  77.5 0.1 copy.49
  77.6 18.3 %all_to_all.23 = bf16[4,128,128]{2,0,1:T(4,128)(2,1)S(1)} all-to-all(bf16[4,128,128]{2,0,1:T(4,128)(2,1)S(1)} %copy.49), channel_id=1, replica_groups=mesh['ctx'=128,'tp'=4] {'ctx'}, dimensions={1} | all-to-all | bytes 262144 | tf_op jit(solution)/shard_map/all_to_all | solution.py:126
  95.9 0.0 copy-done
  95.9 1.3 fusion
  97.2 0.0 reduce-scatter.2.cloned.1.call-update
  97.2 34.2 %reduce-scatter.2.cloned.1.call-done = bf16[512,128]{0,1:T(8,128)(2,1)} async-done(((bf16[2048,128]{0,1:T(8,128)(2,1)}), bf16[512,128]{0,1:T(8,128)(2,1)}) %reduce-scatter.2.cloned.1.call-update) | async-done | bytes 131088 | tf_op jit(solution)/shard_map/reduce_scatter | solution.py:128
  131.4 1.7 %copy.50 = bf16[512,128]{1,0:T(8,128)(2,1)} copy(bf16[512,128]{0,1:T(8,128)(2,1)} %reduce-scatter.2.cloned.1.call-done) | data formatting | bytes 262144 | tf_op jit(solution)/shard_map/reduce_scatter | solution.py:128
  (3 shorter events, 0.1 us)
Async XLA Ops:
  6.5 89.4 %copy-start = (bf16[512,2048]{1,0:T(8,128)(2,1)S(1)}, bf16[512,2048]{1,0:T(8,128)(2,1)}, u32[]{:S(2)}) copy-start(bf16[512,2048]{1,0:T(8,128)(2,1)} %param.9) | copy-start | bytes 6291460
  8.6 12.4 %collective-permute-start = (bf16[3,512,2]{2,1,0:T(8,128)(2,1)}, bf16[3,512,2]{2,1,0:T(8,128)(2,1)S(1)}, u32[]{:S(2)}, u32[]{:S(2)}) collective-permute-start(bf16[3,512,2]{2,1,0:T(8,128)(2,1)} %slice.49), channel_id=1, source_target_pairs={{0,4},{4,8},{8,12},{12,16},{16,20},{20,24},{24,28},{28,32},{32,36}... | collective-permute-start | bytes 18440 | tf_op jit(solution)/shard_map/ppermute | solution.py:14
  12.8 6.4 %copy-start.2 = (f32[128,128]{0,1:T(8,128)}, f32[128,128]{0,1:T(8,128)S(1)}, u32[]{:S(2)}) copy-start(f32[128,128]{0,1:T(8,128)S(1)} %fusion.85) | copy-start | bytes 196612
  13.1 1.8 %copy-start.4 = (f32[128,128]{0,1:T(8,128)}, f32[128,128]{0,1:T(8,128)S(1)}, u32[]{:S(2)}) copy-start(f32[128,128]{0,1:T(8,128)S(1)} %fusion.84) | copy-start | bytes 196612
  14.6 4.6 %copy-start.6 = (f32[1,128,256]{1,2,0:T(8,128)}, f32[1,128,256]{1,2,0:T(8,128)S(1)}, u32[]{:S(2)}) copy-start(f32[1,128,256]{1,2,0:T(8,128)S(1)} %fusion.4) | copy-start | bytes 393220
  14.9 4.3 %copy-start.7 = (f32[1,128,256]{1,2,0:T(8,128)}, f32[1,128,256]{1,2,0:T(8,128)S(1)}, u32[]{:S(2)}) copy-start(f32[1,128,256]{1,2,0:T(8,128)S(1)} %convolution_bitcast_fusion.1) | copy-start | bytes 393220
  16.7 4.3 %copy-start.8 = (f32[3,3,512]{2,1,0:T(4,128)S(1)}, f32[3,3,512]{2,1,0:T(4,128)}, u32[]{:S(2)}) copy-start(f32[3,3,512]{2,1,0:T(4,128)} %param.6) | copy-start | bytes 55300
  16.7 4.3 %copy-start.1 = (bf16[3,512,128]{2,1,0:T(8,128)(2,1)S(1)}, bf16[3,512,128]{2,1,0:T(8,128)(2,1)}, u32[]{:S(2)}) copy-start(bf16[3,512,128]{2,1,0:T(8,128)(2,1)} %param.5) | copy-start | bytes 1179652
  23.3 31.3 %all-to-all-start = ((bf16[128,4,128]{2,1,0:T(4,128)(2,1)}), bf16[128,4,128]{2,1,0:T(4,128)(2,1)S(1)}, u32[]{:S(2)}, u32[]{:S(2)}) async-start(bf16[128,4,128]{2,1,0:T(4,128)(2,1)} %bitcast.4), calls=%async_computation | async-start | bytes 262144 | tf_op jit(solution)/shard_map/all_to_all | solution.py:109
  43.3 88.0 %reduce-scatter.2.cloned.1.call-start = ((), (), s32[]{:S(2)}) async-start(), calls=%async_computation.3 | async-start | bytes 655360 | tf_op jit(solution)/shard_map/reduce_scatter | solution.py:128
  72.4 1.8 %copy-start.3 = (f32[128,128]{0,1:T(8,128)S(1)}, f32[128,128]{0,1:T(8,128)}, u32[]{:S(2)}) copy-start(f32[128,128]{0,1:T(8,128)} %copy-done.2) | copy-start | bytes 196612
  72.4 2.5 %copy-start.5 = (f32[128,128]{0,1:T(8,128)S(1)}, f32[128,128]{0,1:T(8,128)}, u32[]{:S(2)}) copy-start(f32[128,128]{0,1:T(8,128)} %copy-done.4) | copy-start | bytes 196612
Sparse Core Ops, SparseCore 0:
  97.3 34.0 reduce-scatter.1
where the time goes:
time: 140 us
  waiting for transfers between devices  41 us (29%)
  matrix products  30.2 us (22%)
  starting transfers between devices  24.2 us (17%)
  blocking collectives  18.3 us (13%)
  between operations  13.7 us (10%)
  local copies, waits for them, and re-layouts  9.05 us (6%)
  other arithmetic  3.38 us (2%)
    reduce_scatter x1, waiting for transfers between devices, local(): lax.psum_scatter(lax.dot_general(out_weight, gated, (((0,), (0,)), ((), (...  34.2 us
    dot_general x12, matrix products, right_product(): return jnp.einsum('bks,st->bkt', stacked, matrix, precision=highest)  23.5 us
    all_to_all x1, starting transfers between devices, local(): lax.all_to_all(product, 'ctx', split_axis=0, concat_axis=1, tiled=True)  20.1 us
    all_to_all x1, blocking collectives, local(): lax.all_to_all(long_mix, 'ctx', split_axis=1, concat_axis=0, tiled=True)  18.3 us
    all_to_all x1, waiting for transfers between devices, local(): lax.all_to_all(product, 'ctx', split_axis=0, concat_axis=1, tiled=True)  6.82 us
    dot_general x6, matrix products, left_product(): return jnp.einsum('kn,bns->bks', matrix, stacked, precision=highest)  5.45 us
    ppermute x1, starting transfers between devices, from_behind(): lax.ppermute(value, axis, [(source, source + steps) for source in range(i...  3.94 us
  transfers between devices with their start and end apart: 3, of which 2 were waited for; matrix products, arithmetic and copies ran while one was open for 9% of the time, Pallas kernels for 0%

commit v1 on v0

--- a/solution.py
+++ b/solution.py
@@ -6,6 +6,12 @@
 
 GROUP = 16
 highest = lax.Precision.HIGHEST
+
+
+def stacked_exchange(array, mesh_axis, split, join):
+    pieces = jnp.split(array, lax.axis_size(mesh_axis), axis=split)
+    received = lax.all_to_all(jnp.stack(pieces), mesh_axis, 0, 0)
+    return jnp.concatenate(received, axis=join)
 
 
 def from_behind(value, axis, steps):
@@ -106,7 +112,7 @@
         )
     query_conv = conv_all[0]
     product = (conv_all[1] * conv_all[2]).astype(jnp.bfloat16)
-    gathered = lax.all_to_all(product, "ctx", split_axis=0, concat_axis=1, tiled=True)
+    gathered = stacked_exchange(product, "ctx", 0, 1)
     signal = gathered.astype(jnp.float32)
     sig_real, sig_imag = forward_dft(signal.reshape(chan_dev, half_rows, col_count), tables)
     four_shape = (group_dev, per_group, row_count, col_count)

time: 140 us -> 211 us (1.51)
  local copies, waits for them, and re-layouts: 9.05 us -> 80.6 us
    unnamed x18 -> x145, local copies, waits for them, and re-layouts: 0.04 us -> 71.7 us
  transfers between devices with their start and end apart: 3 -> 3, of which waited for: 2 -> 2; matrix products, arithmetic and copies ran while one was open for 9% -> 6% of each run, Pallas kernels for 0% -> 0%
where the time goes in v1:
time: 211 us
  local copies, waits for them, and re-layouts  80.6 us (38%)
  waiting for transfers between devices  41 us (19%)
  matrix products  30.2 us (14%)
  starting transfers between devices  24 us (11%)
  blocking collectives  18.3 us (9%)
  between operations  13.8 us (7%)
  other arithmetic  2.72 us (1%)
    unnamed x145, local copies, waits for them, and re-layouts  71.7 us
    reduce_scatter x1, waiting for transfers between devices, local(): lax.psum_scatter(lax.dot_general(out_weight, gated, (((0,), (0,)), ((), (...  34.2 us
    dot_general x12, matrix products, right_product(): return jnp.einsum('bks,st->bkt', stacked, matrix, precision=highest)  23.5 us
    all_to_all x1, starting transfers between devices, stacked_exchange(): received = lax.all_to_all(jnp.stack(pieces), mesh_axis, 0, 0)  19.8 us
    all_to_all x1, blocking collectives, local(): lax.all_to_all(long_mix, 'ctx', split_axis=1, concat_axis=0, tiled=True)  18.3 us
    all_to_all x1, waiting for transfers between devices, stacked_exchange(): received = lax.all_to_all(jnp.stack(pieces), mesh_axis, 0, 0)  6.83 us
    dot_general x6, matrix products, left_product(): return jnp.einsum('kn,bns->bks', matrix, stacked, precision=highest)  5.45 us
  transfers between devices with their start and end apart: 3, of which 2 were waited for; matrix products, arithmetic and copies ran while one was open for 6% of the time, Pallas kernels for 0%

profile of v1, /device:TPU:1, one launch (start us, length us, event | category | flops | bytes accessed | tf_op | source)
XLA Modules:
  0.0 210.6 jit_solution(17544458526883891699)
XLA Ops:
  6.5 1.3 slice.177
  7.9 4.0 %collective-permute-start = (bf16[3,512,2]{2,1,0:T(8,128)(2,1)S(1)}, bf16[3,512,2]{2,1,0:T(8,128)(2,1)S(1)}, u32[]{:S(2)}, u32[]{:S(2)}) collective-permute-start(bf16[3,512,2]{2,1,0:T(8,128)(2,1)S(1)} %slice.177), channel_id=1, source_target_pairs={{0,4},{4,8},{8,12},{12,16},{16,20},{20,24},{24,28},{28,32},{32,36}... | collective-permute-start | bytes 18440 | tf_op jit(solution)/shard_map/ppermute | solution.py:20
  12.4 1.2 dynamic-slice_reduce_fusion
  14.2 1.8 fusion.46
  16.0 2.5 %fusion.50 = f32[128,256]{1,0:T(8,128)} fusion(f32[1,128,256]{1,2,0:T(8,128)S(1)} %fusion.4, f32[1,128,256]{1,2,0:T(8,128)S(1)} %convolution_bitcast_fusion.1), kind=kOutput, calls=%fused_computation.209 | convolution fusion | flops 102137856 | bytes 393216 | tf_op jit(solution)/shard_map/bks,st->bkt/dot_general | solution.py:28
  18.5 1.8 convolution_subtract_fusion.3
  20.7 1.2 fusion.5
  22.5 0.6 constant_dynamic-update-slice_fusion.126
  23.6 0.6 constant_dynamic-update-slice_fusion.124
  24.7 0.6 constant_dynamic-update-slice_fusion.122
  25.9 0.6 constant_dynamic-update-slice_fusion.120
  27.0 0.6 constant_dynamic-update-slice_fusion.118
  28.1 0.6 constant_dynamic-update-slice_fusion.116
  29.2 0.6 constant_dynamic-update-slice_fusion.114
  30.4 0.6 constant_dynamic-update-slice_fusion.112
  31.5 0.6 constant_dynamic-update-slice_fusion.110
  32.6 0.6 constant_dynamic-update-slice_fusion.108
  33.8 0.6 constant_dynamic-update-slice_fusion.106
  34.9 0.6 constant_dynamic-update-slice_fusion.104
  36.0 0.6 constant_dynamic-update-slice_fusion.102
  37.2 0.6 constant_dynamic-update-slice_fusion.100
  38.3 0.6 constant_dynamic-update-slice_fusion.98
  39.4 0.6 constant_dynamic-update-slice_fusion.96
  40.5 0.6 constant_dynamic-update-slice_fusion.94
  41.7 0.6 constant_dynamic-update-slice_fusion.92
  42.8 0.6 constant_dynamic-update-slice_fusion.90
  43.9 0.6 constant_dynamic-update-slice_fusion.88
  45.1 0.6 constant_dynamic-update-slice_fusion.86
  46.2 0.6 constant_dynamic-update-slice_fusion.84
  47.3 0.6 constant_dynamic-update-slice_fusion.82
  48.5 0.6 constant_dynamic-update-slice_fusion.80
  49.6 0.6 constant_dynamic-update-slice_fusion.78
  50.7 0.6 constant_dynamic-update-slice_fusion.76
  51.8 0.6 constant_dynamic-update-slice_fusion.74
  53.0 0.6 constant_dynamic-update-slice_fusion.72
  54.1 0.6 constant_dynamic-update-slice_fusion.70
  55.2 0.6 constant_dynamic-update-slice_fusion.68
  56.4 0.6 constant_dynamic-update-slice_fusion.66
  57.5 0.6 constant_dynamic-update-slice_fusion.64
  58.6 0.6 constant_dynamic-update-slice_fusion.62
  59.8 0.6 constant_dynamic-update-slice_fusion.60
  94.2 19.8 %all-to-all-start = ((bf16[128,4,128]{2,1,0:T(4,128)(2,1)}), bf16[128,4,128]{2,1,0:T(4,128)(2,1)S(1)}, u32[]{:S(2)}, u32[]{:S(2)}) async-start(bf16[128,4,128]{2,1,0:T(4,128)(2,1)} %constant_dynamic-update-slice_fusion), calls=%async_computation | async-start | bytes 262144 | tf_op jit(solution)/shard_map/all_to_all | solution.py:13
  114.8 0.8 dynamic_slice.7
  115.6 2.8 %convolution_add_fusion.2 = f32[128,256]{1,0:T(8,128)S(1)} fusion(f32[128,256]{1,0:T(8,128)} %fusion.50, f32[1,128,256]{1,2,0:T(8,128)} %copy-done.7, f32[1,128,256]{1,2,0:T(8,128)} %copy-done.6), kind=kOutput, calls=%fused_computation.13 | convolution fusion | flops 102170624 | bytes 524288 | tf_op jit(solution)/shard_map/bks,st->bkt/dot_general | solution.py:28
  118.5 6.8 %all-to-all-done = bf16[128,4,128]{2,1,0:T(4,128)(2,1)S(1)} async-done(((bf16[128,4,128]{2,1,0:T(4,128)(2,1)}), bf16[128,4,128]{2,1,0:T(4,128)(2,1)S(1)}, u32[]{:S(2)}, u32[]{:S(2)}) %all-to-all-start) | async-done | bytes 131104 | tf_op jit(solution)/shard_map/all_to_all | solution.py:13
  125.3 0.7 copy.108
  126.0 1.6 reshape.401
  127.5 1.3 fusion.1
  128.9 1.3 convolution_bitcast_fusion
  130.2 1.9 fusion.28
  132.1 1.9 fusion.30
  134.0 1.9 convolution_subtract_fusion.1
  135.9 1.9 convolution_add_fusion.1
  137.8 1.9 fusion.24
  139.7 1.7 fusion.26
  141.4 1.7 convolution_add_fusion
  143.2 1.7 convolution_subtract_fusion
  144.9 0.8 fusion.10
  145.7 1.5 fusion.3
  147.1 1.0 reshape.405
  148.3 18.3 %all_to_all.15 = bf16[4,128,128]{2,0,1:T(4,128)(2,1)S(1)} all-to-all(bf16[4,128,128]{2,0,1:T(4,128)(2,1)S(1)} %copy.89), channel_id=1, replica_groups=mesh['ctx'=128,'tp'=4] {'ctx'}, dimensions={1} | all-to-all | bytes 262144 | tf_op jit(solution)/shard_map/all_to_all | solution.py:132
  166.6 1.3 fusion
  167.9 34.2 %reduce-scatter.2.cloned.1.call-done = bf16[512,128]{0,1:T(8,128)(2,1)} async-done(((bf16[2048,128]{0,1:T(8,128)(2,1)}), bf16[512,128]{0,1:T(8,128)(2,1)}) %reduce-scatter.2.cloned.1.call-update) | async-done | bytes 131088 | tf_op jit(solution)/shard_map/reduce_scatter | solution.py:134
  202.1 1.7 copy.90
  (127 shorter events, 55.5 us)
Async XLA Ops:
  6.5 160.1 %copy-start = (bf16[512,2048]{1,0:T(8,128)(2,1)S(1)}, bf16[512,2048]{1,0:T(8,128)(2,1)}, u32[]{:S(2)}) copy-start(bf16[512,2048]{1,0:T(8,128)(2,1)} %param.9) | copy-start | bytes 6291460
  7.9 12.5 %collective-permute-start = (bf16[3,512,2]{2,1,0:T(8,128)(2,1)S(1)}, bf16[3,512,2]{2,1,0:T(8,128)(2,1)S(1)}, u32[]{:S(2)}, u32[]{:S(2)}) collective-permute-start(bf16[3,512,2]{2,1,0:T(8,128)(2,1)S(1)} %slice.177), channel_id=1, source_target_pairs={{0,4},{4,8},{8,12},{12,16},{16,20},{20,24},{24,28},{28,32},{32,36}... | collective-permute-start | bytes 18440 | tf_op jit(solution)/shard_map/ppermute | solution.py:20
  12.1 2.0 copy-start.2
  12.4 1.8 copy-start.4
  13.9 4.6 %copy-start.6 = (f32[1,128,256]{1,2,0:T(8,128)}, f32[1,128,256]{1,2,0:T(8,128)S(1)}, u32[]{:S(2)}) copy-start(f32[1,128,256]{1,2,0:T(8,128)S(1)} %fusion.4) | copy-start | bytes 393220
  14.2 4.3 %copy-start.7 = (f32[1,128,256]{1,2,0:T(8,128)}, f32[1,128,256]{1,2,0:T(8,128)S(1)}, u32[]{:S(2)}) copy-start(f32[1,128,256]{1,2,0:T(8,128)S(1)} %convolution_bitcast_fusion.1) | copy-start | bytes 393220
  16.0 4.3 %copy-start.8 = (f32[3,3,512]{2,1,0:T(4,128)S(1)}, f32[3,3,512]{2,1,0:T(4,128)}, u32[]{:S(2)}) copy-start(f32[3,3,512]{2,1,0:T(4,128)} %param.6) | copy-start | bytes 55300
  16.0 4.3 %copy-start.1 = (bf16[3,512,128]{2,1,0:T(8,128)(2,1)S(1)}, bf16[3,512,128]{2,1,0:T(8,128)(2,1)}, u32[]{:S(2)}) copy-start(bf16[3,512,128]{2,1,0:T(8,128)(2,1)} %param.5) | copy-start | bytes 1179652
  94.2 31.1 %all-to-all-start = ((bf16[128,4,128]{2,1,0:T(4,128)(2,1)}), bf16[128,4,128]{2,1,0:T(4,128)(2,1)S(1)}, u32[]{:S(2)}, u32[]{:S(2)}) async-start(bf16[128,4,128]{2,1,0:T(4,128)(2,1)} %constant_dynamic-update-slice_fusion), calls=%async_computation | async-start | bytes 262144 | tf_op jit(solution)/shard_map/all_to_all | solution.py:13
  114.1 88.0 %reduce-scatter.2.cloned.1.call-start = ((), (), s32[]{:S(2)}) async-start(), calls=%async_computation.3 | async-start | bytes 655360 | tf_op jit(solution)/shard_map/reduce_scatter | solution.py:134
  143.1 1.8 copy-start.3
  143.1 2.5 %copy-start.5 = (f32[128,128]{0,1:T(8,128)S(1)}, f32[128,128]{0,1:T(8,128)}, u32[]{:S(2)}) copy-start(f32[128,128]{0,1:T(8,128)} %copy-done.4) | copy-start | bytes 196612
Sparse Core Ops, SparseCore 0:
  168.0 34.0 reduce-scatter.1
